TPU v7x, 32 devices: a whole 2x2x4 slice. The times are simulated.
32 devices in a mesh: gx: 4 (over y, x), gy: 2 (over core), gz: 4 (over z).
Axes of the slice: x: 2, y: 2, z: 4, core: 2. Of those that a mesh axis runs over, the one named last changes fastest.
Arguments:
- field: bfloat16 [16, 64, 32, 512], P(None, 'gz', 'gy', 'gx'), may hold values from -6 to 6
- fine_taps: float32 [3, 9], replicated, may hold values from 0.1 to 0.6
- coarse_taps: float32 [3, 9], replicated, may hold values from 0.1 to 0.6
- top_kernel: bfloat16 [8, 4, 64, 2048], P('gz', 'gy', 'gx'), may hold values from -6 to 6
Outputs:
- applied: bfloat16 [16, 64, 32, 512], P(None, 'gz', 'gy', 'gx')
All inputs are finite; a program needn't handle non-finite values.
Results may differ from a plain program's by a relative error of at most 0.0047.
Values may be sent and summed in bfloat16 or wider, within the bound.
No kernel may reach another device: no remote copies, remote signals or barrier semaphores. Data moves between devices by JAX's collectives and lax.ppermute only.
A program may use at most 128 MiB of HBM per device.

v0:
```python
import jax
import jax.numpy as jnp
from jax import lax
from jax.sharding import PartitionSpec as P


def padded_2(cells, sides, width):
    for axis, dim in sides:
        count = lax.axis_size(axis)
        ends = count - 1
        head = lax.slice_in_dim(cells, 0, width, axis=dim)
        tail = lax.slice_in_dim(cells, cells.shape[dim] - width, cells.shape[dim], axis=dim)
        cells = jnp.concatenate(
            [
                lax.ppermute(tail, axis, [(i, (i + 1) % count) for i in range(ends)]),
                cells,
                lax.ppermute(head, axis, [((i + 1) % count, i) for i in range(ends)]),
            ],
            axis=dim,
        )
    return cells


def band_matrix(kernel_row, padded_length):
    length = padded_length - 8
    source = lax.broadcasted_iota(jnp.int32, (padded_length, length), 0)
    target = lax.broadcasted_iota(jnp.int32, (padded_length, length), 1)
    offset = source - target
    band = jnp.zeros((padded_length, length), jnp.float32)
    for tap in range(9):
        band = band + jnp.where(offset == tap, kernel_row[tap], 0.0)
    return band


def conv_padded(padded, kernel_row, along):
    length = padded.shape[along] - 8
    if along == padded.ndim - 1:
        band = band_matrix(kernel_row, padded.shape[along])
        return lax.dot_general(
            padded,
            band,
            (((along,), (0,)), ((), ())),
            precision=lax.Precision.HIGHEST,
            preferred_element_type=jnp.float32,
        )
    total = kernel_row[0] * lax.slice_in_dim(padded, 0, length, axis=along)
    for offset in range(1, 9):
        total = total + kernel_row[offset] * lax.slice_in_dim(
            padded, offset, offset + length, axis=along
        )
    return total


def separable_steps(values, kernel, rim_x, rim_y, rim_z):
    values = conv_padded(rim_x(values).astype(jnp.float32), kernel[2], 3)
    values = conv_padded(rim_y(values), kernel[1], 2)
    return conv_padded(rim_z(values), kernel[0], 1)


def restrict(values, factor):
    count, depth, rows, cols = values.shape
    shaped = values.reshape(
        count, depth // factor, factor, rows // factor, factor, cols // factor, factor
    )
    return shaped.mean(axis=(2, 4, 6))


def prolong(values, factor):
    values = jnp.repeat(values, factor, axis=1)
    values = jnp.repeat(values, factor, axis=2)
    return jnp.repeat(values, factor, axis=3)


def shards(field, fine_taps, coarse_taps, top_kernel):
    cells = field.astype(jnp.float32)
    coarse_cells = restrict(cells, 2)
    fine_part = separable_steps(
        field,
        fine_taps,
        lambda values: padded_2(values, (("gx", 3),), 4),
        lambda values: padded_2(values, (("gy", 2),), 4),
        lambda values: padded_2(values, (("gz", 1),), 4),
    )
    coarse_part = separable_steps(
        coarse_cells,
        coarse_taps,
        lambda values: padded_2(values.astype(jnp.bfloat16), (("gx", 3),), 4).astype(values.dtype),
        lambda values: padded_2(values.astype(jnp.bfloat16), (("gy", 2),), 4).astype(values.dtype),
        lambda values: padded_2(values.astype(jnp.bfloat16), (("gz", 1),), 4).astype(values.dtype),
    )
    top_in = restrict(coarse_cells, 4).astype(jnp.bfloat16)
    count, top_depth, top_rows, top_cols = top_in.shape
    along_x = lax.all_gather(top_in, "gx", axis=3, tiled=True)
    along_y = lax.all_gather(along_x, "gy", axis=2, tiled=True)
    along_z = lax.all_gather(along_y, "gz", axis=1, tiled=True)
    whole_top = along_z.reshape(count, -1)
    kernel_rows = top_kernel.reshape(-1, top_kernel.shape[3])
    top_part = lax.dot_general(
        whole_top, kernel_rows, (((1,), (1,)), ((), ())), preferred_element_type=jnp.float32
    )
    top_part = top_part.reshape(count, top_depth, top_rows, top_cols)
    coarse_total = coarse_part + prolong(top_part, 4)
    return (fine_part + prolong(coarse_total, 2)).astype(jnp.bfloat16)


def solution(mesh):
    return jax.shard_map(
        shards,
        mesh=mesh,
        in_specs=(P(None, "gz", "gy", "gx"), P(), P(), P("gz", "gy", "gx", None)),
        out_specs=P(None, "gz", "gy", "gx"),
        check_vma=False,
    )
```

profile of v0, /device:TPU:0, one launch (start us, length us, event | category | flops | bytes accessed | tf_op | source)
XLA Modules:
  0.0 185.4 jit_solution(7652606793168775549)
XLA Ops:
  0.0 9.9 %copy.23 = f32[16,16,16,128]{0,3,2,1:T(8,128)} copy(bf16[16,16,16,128]{3,2,1,0:T(8,128)(2,1)} %param.4) | data formatting | bytes 3145728 | tf_op jit(solution)/shard_map/reshape | solution.py:62
  9.9 11.7 %reduce_sum.18 = f32[16,8,8,64]{0,3,2,1:T(8,128)S(1)} reduce(f32[16,8,2,8,2,64,2]{0,6,5,4,3,2,1:T(2,128)} %bitcast.77, f32[]{:T(128)} %constant.13.clone.1), dimensions={2,4,6}, to_apply=%region_0.0 | reduce | flops 458752 | bytes 2359300 | tf_op jit(solution)/shard_map/reduce_sum | solution.py:65
  21.7 0.0 copy-start.2
  21.7 1.4 copy.24
  23.1 1.9 %fusion.209 = (bf16[16,8,8,64]{3,0,2,1:T(8,128)(2,1)S(1)}, f32[16,8,8,64]{3,0,2,1:T(8,128)}) fusion(f32[16,8,8,64]{3,0,2,1:T(8,128)} %copy.24), kind=kLoop, calls=%fused_computation.244 | loop fusion | flops 131072 | bytes 655360 | tf_op jit(solution)/shard_map/convert_element_type | solution.py:87
  25.0 0.7 copy-done.3
  25.7 0.9 fusion.215
  26.6 5.6 %collective-permute-start.6 = (bf16[16,8,8,4]{3,0,2,1:T(8,128)(2,1)}, bf16[16,8,8,4]{3,0,2,1:T(8,128)(2,1)}, u32[]{:S(2)}, u32[]{:S(2)}) collective-permute-start(bf16[16,8,8,4]{3,0,2,1:T(8,128)(2,1)} %get-tuple-element.17), channel_id=1, source_target_pairs={{0,8},{8,16},{16,24},{1,9},{9,17},{17,25},{2,10},{10,18},{18,26},{... | collective-permute-start | bytes 24584 | tf_op jit(solution)/shard_map/ppermute | solution.py:15
  32.1 1.3 collective-permute-start.7
  33.4 0.6 fusion.212
  34.0 0.0 copy-start.4
  34.0 0.0 copy-start.5
  34.0 2.5 %copy.37 = bf16[16,16,16,4]{2,1,3,0:T(8,128)(2,1)} copy(bf16[16,16,16,4]{3,2,1,0:T(8,128)(2,1)S(1)} %get-tuple-element.9) | data formatting | bytes 65536
  36.5 5.2 %collective-permute-start = (bf16[16,16,16,4]{2,1,3,0:T(8,128)(2,1)}, bf16[16,16,16,4]{2,1,3,0:T(8,128)(2,1)}, u32[]{:S(2)}, u32[]{:S(2)}) collective-permute-start(bf16[16,16,16,4]{2,1,3,0:T(8,128)(2,1)} %copy.37), channel_id=1, source_target_pairs={{0,8},{8,16},{16,24},{1,9},{9,17},{17,25},{2,10},{10,18},{18,26},{... | collective-permute-start | bytes 98312 | tf_op jit(solution)/shard_map/ppermute | solution.py:15
  41.7 2.5 %copy.38 = bf16[16,16,16,4]{2,1,3,0:T(8,128)(2,1)} copy(bf16[16,16,16,4]{3,2,1,0:T(8,128)(2,1)S(1)} %get-tuple-element.10) | data formatting | bytes 65536
  44.2 1.3 collective-permute-start.1
  45.5 0.7 fusion.218
  46.2 0.7 fusion.219
  46.9 0.7 fusion.216
  47.6 0.7 fusion.217
  48.3 1.7 copy.25
  49.9 0.5 reduce_sum.19
  50.5 9.9 %all_gather.9 = bf16[16,2,2,64]{0,2,1,3:T(2,128)(2,1)S(1)} all-gather(bf16[16,2,2,16]{0,2,1,3:T(2,128)(2,1)S(1)} %copy.26), channel_id=1, replica_groups=mesh['gx'=4,'gy'=2,'gz'=4] {'gx'}, dimensions={3}, use_global_device_ids=true | all-gather | bytes 10240 | tf_op jit(solution)/shard_map/all_gather | solution.py:93
  60.4 0.1 copy.27
  60.5 1.8 all_gather.10
  62.3 13.6 %all_gather.11 = bf16[16,8,4,64]{3,0,1,2:T(8,128)(2,1)S(1)} all-gather(bf16[16,2,4,64]{3,0,1,2:T(8,128)(2,1)S(1)} %all_gather.10), channel_id=1, replica_groups=mesh['gx'=4,'gy'=2,'gz'=4] {'gz'}, dimensions={1}, use_global_device_ids=true | all-gather | bytes 81920 | tf_op jit(solution)/shard_map/all_gather | solution.py:95
  75.9 0.1 copy.28
  76.0 0.2 reshape.156
  76.2 0.0 collective-permute-done.7
  76.2 7.2 %convolution_convert_fusion = bf16[16,8,8,64]{3,0,2,1:T(8,128)(2,1)S(1)} fusion(bf16[16,8,8,4]{3,0,2,1:T(8,128)(2,1)} %collective-permute-done.7, bf16[16,8,8,64]{3,0,2,1:T(8,128)(2,1)} %copy-done.3, bf16[16,8,8,4]{3,0,2,1:T(8,128)(2,1)} %collective-permute-done.6, f32[]{:T(128)} %bitcast.40, f32[]{:T(128)} %bitcast.39, f32[]{:T(128)} %bitcast.38, ...), kind=kOutput, calls=%fused_computation.80 | convolution fusion | flops 57255424 | bytes 278564 | tf_op jit(solution)/shard_map/dot_general | solution.py:39
  83.4 1.3 collective-permute-start.8
  84.7 1.3 collective-permute-start.9
  86.0 0.0 collective-permute-done
  86.0 2.5 %copy.21 = bf16[16,16,16,4]{3,2,1,0:T(8,128)(2,1)S(1)} copy(bf16[16,16,16,4]{2,1,3,0:T(8,128)(2,1)} %collective-permute-done) | data formatting | bytes 65536 | tf_op jit(solution)/shard_map/ppermute | solution.py:15
  88.6 3.5 %copy.22 = bf16[16,16,16,4]{3,2,1,0:T(8,128)(2,1)} copy(bf16[16,16,16,4]{2,1,3,0:T(8,128)(2,1)} %collective-permute-done.1) | data formatting | bytes 65536 | tf_op jit(solution)/shard_map/ppermute | solution.py:17
  92.0 9.0 %fusion.46 = f32[16,16,16,128]{3,2,1,0:T(8,128)S(1)} fusion(bf16[16,16,16,4]{3,2,1,0:T(8,128)(2,1)} %copy.22, bf16[16,16,16,128]{3,2,1,0:T(8,128)(2,1)S(1)} %copy-done.2, bf16[16,16,16,4]{3,2,1,0:T(8,128)(2,1)S(1)} %copy.21, f32[]{:T(128)} %bitcast.10, f32[]{:T(128)} %bitcast.9, f32[]{:T(128)} %bitcast.8, f32[]{:T(128)} %bitcast.7, f32[]{:T(128)} %bitcast.6, ...), kind=kOutput, calls=%fused_computation.74 | convolution fusion | flops 859450368 | bytes 3211300 | tf_op jit(solution)/shard_map/dot_general | solution.py:39
  101.1 0.2 fusion.211
  101.3 3.1 %collective-permute-start.2 = (f32[16,16,4,128]{3,2,1,0:T(4,128)S(1)}, f32[16,16,4,128]{3,2,1,0:T(4,128)S(1)}, u32[]{:S(2)}, u32[]{:S(2)}) collective-permute-start(f32[16,16,4,128]{3,2,1,0:T(4,128)S(1)} %get-tuple-element.7), channel_id=1, source_target_pairs={{0,4},{1,5},{2,6},{3,7},{8,12},{9,13},{10,14},{11,15},{16,20},{17,... | collective-permute-start | bytes 1572872 | tf_op jit(solution)/shard_map/ppermute | solution.py:15
  104.3 1.5 collective-permute-start.3
  105.9 0.2 maximum_convert_fusion
  106.0 5.7 %fusion.62 = bf16[16,8,8,64]{3,0,2,1:T(8,128)(2,1)S(1)} fusion(f32[16,8,16,64]{3,0,2,1:T(8,128)S(1)} %maximum_convert_fusion, f32[]{:T(128)} %bitcast.50, f32[]{:T(128)} %bitcast.49, f32[]{:T(128)} %bitcast.48, f32[]{:T(128)} %bitcast.47, f32[]{:T(128)} %bitcast.46, f32[]{:T(128)} %bitcast.45, f32[]{:T(128)} %bitcast.44, f32[]{:T(128)} %bitcast.43, f32[]{:T(128)} %bitcast.30), kind=kLoop, calls=%fused_computation.101 | loop fusion | flops 1179648 | bytes 2490404 | tf_op jit(solution)/shard_map/convert_element_type | solution.py:89
  111.7 0.7 fusion.213
  112.4 3.5 %collective-permute-start.10 = (bf16[16,4,8,64]{3,0,2,1:T(8,128)(2,1)}, bf16[16,4,8,64]{3,0,2,1:T(8,128)(2,1)S(1)}, u32[]{:S(2)}, u32[]{:S(2)}) collective-permute-start(bf16[16,4,8,64]{3,0,2,1:T(8,128)(2,1)} %get-tuple-element.13), channel_id=1, source_target_pairs={{0,1},{1,2},{2,3},{4,5},{5,6},{6,7},{8,9},{9,10},{10,11},{12,13},{... | collective-permute-start | bytes 196616 | tf_op jit(solution)/shard_map/ppermute | solution.py:15
  115.9 1.3 collective-permute-start.11
  117.3 8.9 %fusion.25 = f32[16,16,16,128]{3,2,1,0:T(8,128)S(1)} fusion(f32[16,16,16,128]{3,2,1,0:T(8,128)S(1)} %fusion.46, f32[16,16,4,128]{3,2,1,0:T(4,128)S(1)} %collective-permute-done.3, f32[16,16,4,128]{3,2,1,0:T(4,128)S(1)} %collective-permute-done.2, f32[]{:T(128)} %bitcast.20, f32[]{:T(128)} %bitcast.19, f32[]{:T(128)} %bitcast.18, f32[]{:T(128)} %bitcast.17, ...), kind=kLoop, calls=%fused_computation.49 | loop fusion | flops 13107200 | bytes 5242916 | tf_op jit(solution)/shard_map/add | solution.py:48
  126.2 1.0 fusion.210
  127.2 5.3 %collective-permute-start.4 = (f32[16,4,16,128]{3,2,1,0:T(8,128)}, f32[16,4,16,128]{3,2,1,0:T(8,128)}, u32[]{:S(2)}, u32[]{:S(2)}) collective-permute-start(f32[16,4,16,128]{3,2,1,0:T(8,128)} %get-tuple-element.5), channel_id=1, source_target_pairs={{0,1},{1,2},{2,3},{4,5},{5,6},{6,7},{8,9},{9,10},{10,11},{12,13},{... | collective-permute-start | bytes 1572872 | tf_op jit(solution)/shard_map/ppermute | solution.py:15
  132.6 1.3 collective-permute-start.5
  133.9 0.4 fusion.111
  134.3 0.1 copy.29
  134.4 0.1 broadcast_in_dim.118
  134.4 0.1 broadcast_in_dim.119
  134.5 1.5 broadcast_in_dim.120
  136.0 2.2 %copy.30 = f32[16,8,8,64]{3,0,2,1:T(8,128)S(1)} copy(f32[16,8,8,64]{0,2,3,1:T(8,128)} %bitcast.79) | data formatting | bytes 524288 | tf_op jit(solution)/shard_map/reshape | solution.py:71
  138.2 0.0 collective-permute-done.11
  138.2 0.2 maximum_convert_fusion.1
  138.4 5.9 %fusion.53 = f32[16,8,8,64]{3,0,2,1:T(8,128)S(1)} fusion(f32[16,8,8,64]{3,0,2,1:T(8,128)S(1)} %copy.30, f32[16,16,8,64]{3,0,2,1:T(8,128)S(1)} %maximum_convert_fusion.1, f32[]{:T(128)} %bitcast.58, f32[]{:T(128)} %bitcast.57, f32[]{:T(128)} %bitcast.56, f32[]{:T(128)} %bitcast.55, f32[]{:T(128)} %bitcast.54, f32[]{:T(128)} %bitcast.53, f32[]{:T(128)} %bitcast.52, ...), kind=kLoop, calls=%fused_computation.83 | loop fusion | flops 1179648 | bytes 2883620 | tf_op jit(solution)/shard_map/add | solution.py:102
  144.2 0.3 copy.31
  144.5 0.4 broadcast_in_dim.121
  144.9 1.5 broadcast_in_dim.122
  146.4 6.7 %copy.32 = f32[16,16,16,64]{2,1,3,0:T(8,128)} copy(f32[16,16,16,64]{3,1,2,0:T(8,128)} %bitcast.80) | data formatting | bytes 2097152 | tf_op jit(solution)/shard_map/reshape | solution.py:70
  153.1 10.7 %broadcast_in_dim.123 = f32[16,16,16,64,2]{2,1,4,3,0:T(8,128)} broadcast(f32[16,16,16,64]{2,1,3,0:T(8,128)} %copy.32), dimensions={0,1,2,3} | broadcast | bytes 3145728 | tf_op jit(solution)/shard_map/broadcast_in_dim | solution.py:71
  163.8 11.4 %copy.33 = f32[16,16,16,128]{3,2,1,0:T(8,128)} copy(f32[16,16,16,128]{2,1,3,0:T(8,128)} %bitcast.76) | data formatting | bytes 4194304 | tf_op jit(solution)/shard_map/reshape | solution.py:71
  175.2 10.1 %fusion.5 = bf16[16,16,16,128]{3,2,1,0:T(8,128)(2,1)} fusion(f32[16,16,16,128]{3,2,1,0:T(8,128)} %copy.33, f32[16,16,16,128]{3,2,1,0:T(8,128)S(1)} %fusion.25, f32[16,4,16,128]{3,2,1,0:T(8,128)} %collective-permute-done.5, f32[16,4,16,128]{3,2,1,0:T(8,128)} %collective-permute-done.4, f32[]{:T(128)} %bitcast.28, f32[]{:T(128)} %bitcast.27, f32[]{:T(128)} %bitcast.26, ...), kind=kLoop, calls=%fused_computation.29 | loop fusion | flops 14155776 | bytes 6291492 | tf_op jit(solution)/shard_map/convert_element_type | solution.py:103
  (20 shorter events, 0.1 us)
Async XLA Ops:
  0.0 133.9 %copy-start = (bf16[2,2,16,2048]{3,2,1,0:T(8,128)(2,1)S(1)}, bf16[2,2,16,2048]{3,2,1,0:T(8,128)(2,1)}, u32[]{:S(2)}) copy-start(bf16[2,2,16,2048]{3,2,1,0:T(8,128)(2,1)} %param.7) | copy-start | bytes 786436
  21.7 11.8 %copy-start.2 = (bf16[16,16,16,128]{3,2,1,0:T(8,128)(2,1)S(1)}, bf16[16,16,16,128]{3,2,1,0:T(8,128)(2,1)}, u32[]{:S(2)}) copy-start(bf16[16,16,16,128]{3,2,1,0:T(8,128)(2,1)} %param.4) | copy-start | bytes 3145732
  25.0 0.7 copy-start.3
  26.6 49.6 %collective-permute-start.6 = (bf16[16,8,8,4]{3,0,2,1:T(8,128)(2,1)}, bf16[16,8,8,4]{3,0,2,1:T(8,128)(2,1)}, u32[]{:S(2)}, u32[]{:S(2)}) collective-permute-start(bf16[16,8,8,4]{3,0,2,1:T(8,128)(2,1)} %get-tuple-element.17), channel_id=1, source_target_pairs={{0,8},{8,16},{16,24},{1,9},{9,17},{17,25},{2,10},{10,18},{18,26},{... | collective-permute-start | bytes 24584 | tf_op jit(solution)/shard_map/ppermute | solution.py:15
  32.1 44.1 %collective-permute-start.7 = (bf16[16,8,8,4]{3,0,2,1:T(8,128)(2,1)}, bf16[16,8,8,4]{3,0,2,1:T(8,128)(2,1)}, u32[]{:S(2)}, u32[]{:S(2)}) collective-permute-start(bf16[16,8,8,4]{3,0,2,1:T(8,128)(2,1)} %get-tuple-element.18), channel_id=1, source_target_pairs={{8,0},{16,8},{24,16},{9,1},{17,9},{25,17},{10,2},{18,10},{26,18},{... | collective-permute-start | bytes 24584 | tf_op jit(solution)/shard_map/ppermute | solution.py:17
  34.0 11.5 %copy-start.4 = (f32[3,9]{1,0:T(4,128)S(1)}, f32[3,9]{1,0:T(4,128)}, u32[]{:S(2)}) copy-start(f32[3,9]{1,0:T(4,128)} %param.6) | copy-start | bytes 328
  34.0 12.9 %copy-start.5 = (f32[3,9]{1,0:T(4,128)S(1)}, f32[3,9]{1,0:T(4,128)}, u32[]{:S(2)}) copy-start(f32[3,9]{1,0:T(4,128)} %param.5) | copy-start | bytes 328
  36.5 49.5 %collective-permute-start = (bf16[16,16,16,4]{2,1,3,0:T(8,128)(2,1)}, bf16[16,16,16,4]{2,1,3,0:T(8,128)(2,1)}, u32[]{:S(2)}, u32[]{:S(2)}) collective-permute-start(bf16[16,16,16,4]{2,1,3,0:T(8,128)(2,1)} %copy.37), channel_id=1, source_target_pairs={{0,8},{8,16},{16,24},{1,9},{9,17},{17,25},{2,10},{10,18},{18,26},{... | collective-permute-start | bytes 98312 | tf_op jit(solution)/shard_map/ppermute | solution.py:15
  44.2 44.4 %collective-permute-start.1 = (bf16[16,16,16,4]{2,1,3,0:T(8,128)(2,1)}, bf16[16,16,16,4]{2,1,3,0:T(8,128)(2,1)}, u32[]{:S(2)}, u32[]{:S(2)}) collective-permute-start(bf16[16,16,16,4]{2,1,3,0:T(8,128)(2,1)} %copy.38), channel_id=1, source_target_pairs={{8,0},{16,8},{24,16},{9,1},{17,9},{25,17},{10,2},{18,10},{26,18},{... | collective-permute-start | bytes 98312 | tf_op jit(solution)/shard_map/ppermute | solution.py:17
  83.4 22.4 %collective-permute-start.8 = (bf16[16,8,4,64]{3,0,2,1:T(8,128)(2,1)S(1)}, bf16[16,8,4,64]{3,0,2,1:T(8,128)(2,1)S(1)}, u32[]{:S(2)}, u32[]{:S(2)}) collective-permute-start(bf16[16,8,4,64]{3,0,2,1:T(8,128)(2,1)S(1)} %get-tuple-element.15), channel_id=1, source_target_pairs={{0,4},{1,5},{2,6},{3,7},{8,12},{9,13},{10,14},{11,15},{16,20},{17,... | collective-permute-start | bytes 196616 | tf_op jit(solution)/shard_map/ppermute | solution.py:15
  84.7 21.1 %collective-permute-start.9 = (bf16[16,8,4,64]{3,0,2,1:T(8,128)(2,1)S(1)}, bf16[16,8,4,64]{3,0,2,1:T(8,128)(2,1)S(1)}, u32[]{:S(2)}, u32[]{:S(2)}) collective-permute-start(bf16[16,8,4,64]{3,0,2,1:T(8,128)(2,1)S(1)} %get-tuple-element.16), channel_id=1, source_target_pairs={{4,0},{5,1},{6,2},{7,3},{12,8},{13,9},{14,10},{15,11},{20,16},{21,... | collective-permute-start | bytes 196616 | tf_op jit(solution)/shard_map/ppermute | solution.py:17
  101.3 16.0 %collective-permute-start.2 = (f32[16,16,4,128]{3,2,1,0:T(4,128)S(1)}, f32[16,16,4,128]{3,2,1,0:T(4,128)S(1)}, u32[]{:S(2)}, u32[]{:S(2)}) collective-permute-start(f32[16,16,4,128]{3,2,1,0:T(4,128)S(1)} %get-tuple-element.7), channel_id=1, source_target_pairs={{0,4},{1,5},{2,6},{3,7},{8,12},{9,13},{10,14},{11,15},{16,20},{17,... | collective-permute-start | bytes 1572872 | tf_op jit(solution)/shard_map/ppermute | solution.py:15
  104.3 12.9 %collective-permute-start.3 = (f32[16,16,4,128]{3,2,1,0:T(4,128)S(1)}, f32[16,16,4,128]{3,2,1,0:T(4,128)S(1)}, u32[]{:S(2)}, u32[]{:S(2)}) collective-permute-start(f32[16,16,4,128]{3,2,1,0:T(4,128)S(1)} %get-tuple-element.8), channel_id=1, source_target_pairs={{4,0},{5,1},{6,2},{7,3},{12,8},{13,9},{14,10},{15,11},{20,16},{21,... | collective-permute-start | bytes 1572872 | tf_op jit(solution)/shard_map/ppermute | solution.py:17
  112.4 25.8 %collective-permute-start.10 = (bf16[16,4,8,64]{3,0,2,1:T(8,128)(2,1)}, bf16[16,4,8,64]{3,0,2,1:T(8,128)(2,1)S(1)}, u32[]{:S(2)}, u32[]{:S(2)}) collective-permute-start(bf16[16,4,8,64]{3,0,2,1:T(8,128)(2,1)} %get-tuple-element.13), channel_id=1, source_target_pairs={{0,1},{1,2},{2,3},{4,5},{5,6},{6,7},{8,9},{9,10},{10,11},{12,13},{... | collective-permute-start | bytes 196616 | tf_op jit(solution)/shard_map/ppermute | solution.py:15
  115.9 22.3 %collective-permute-start.11 = (bf16[16,4,8,64]{3,0,2,1:T(8,128)(2,1)S(1)}, bf16[16,4,8,64]{3,0,2,1:T(8,128)(2,1)S(1)}, u32[]{:S(2)}, u32[]{:S(2)}) collective-permute-start(bf16[16,4,8,64]{3,0,2,1:T(8,128)(2,1)S(1)} %get-tuple-element.14), channel_id=1, source_target_pairs={{1,0},{2,1},{3,2},{5,4},{6,5},{7,6},{9,8},{10,9},{11,10},{13,12},{... | collective-permute-start | bytes 196616 | tf_op jit(solution)/shard_map/ppermute | solution.py:17
  127.2 47.9 %collective-permute-start.4 = (f32[16,4,16,128]{3,2,1,0:T(8,128)}, f32[16,4,16,128]{3,2,1,0:T(8,128)}, u32[]{:S(2)}, u32[]{:S(2)}) collective-permute-start(f32[16,4,16,128]{3,2,1,0:T(8,128)} %get-tuple-element.5), channel_id=1, source_target_pairs={{0,1},{1,2},{2,3},{4,5},{5,6},{6,7},{8,9},{9,10},{10,11},{12,13},{... | collective-permute-start | bytes 1572872 | tf_op jit(solution)/shard_map/ppermute | solution.py:15
  132.6 42.6 %collective-permute-start.5 = (f32[16,4,16,128]{3,2,1,0:T(8,128)}, f32[16,4,16,128]{3,2,1,0:T(8,128)}, u32[]{:S(2)}, u32[]{:S(2)}) collective-permute-start(f32[16,4,16,128]{3,2,1,0:T(8,128)} %get-tuple-element.6), channel_id=1, source_target_pairs={{1,0},{2,1},{3,2},{5,4},{6,5},{7,6},{9,8},{10,9},{11,10},{13,12},{... | collective-permute-start | bytes 1572872 | tf_op jit(solution)/shard_map/ppermute | solution.py:17
  175.2 10.1 %copy-start.1 = (bf16[2,2,16,2048]{3,2,1,0:T(8,128)(2,1)S(1)}, bf16[2,2,16,2048]{3,2,1,0:T(8,128)(2,1)}, u32[]{:S(2)}) copy-start(bf16[2,2,16,2048]{3,2,1,0:T(8,128)(2,1)} %param.7) | copy-start | bytes 786436
where the time goes:
time: 187 us; the launch traced here: 185 us
  local copies, waits for them, and re-layouts  66 us (35%)
  other arithmetic  45.1 us (24%)
  starting transfers between devices  31.9 us (17%)
  blocking collectives  25.3 us (14%)
  matrix products  16.6 us (9%)
    ppermute x6, starting transfers between devices, padded_2(): lax.ppermute(tail, axis, [(i, (i + 1) % count) for i in range(ends)])  24 us
    dot_general x2, matrix products, conv_padded(): lax.dot_general(padded, band, (((along,), (0,)), ((), ())), precision=lax...  16.2 us
    all_gather x1, blocking collectives, shards(): along_z = lax.all_gather(along_y, 'gz', axis=1, tiled=True)  13.6 us
    reshape x2, local copies, waits for them, and re-layouts, prolong(): return jnp.repeat(values, factor, axis=3)  13.6 us
    reduce_sum x2, other arithmetic, restrict(): return shaped.mean(axis=(2, 4, 6))  12.3 us
    broadcast_in_dim x2, local copies, waits for them, and re-layouts, prolong(): return jnp.repeat(values, factor, axis=3)  12.1 us
    convert_element_type x1, other arithmetic, shards(): return (fine_part + prolong(coarse_total, 2)).astype(jnp.bfloat16)  10.1 us
    reshape x1, local copies, waits for them, and re-layouts, restrict(): values.reshape(count, depth // factor, factor, rows // factor, factor, co...  9.92 us
  transfers between devices with their start and end apart: 12, of which 0 were waited for; matrix products, arithmetic and copies ran while one was open for 49% of the time, Pallas kernels for 0%

commit v1 on v0

--- a/solution.py
+++ b/solution.py
@@ -2,6 +2,17 @@
 import jax.numpy as jnp
 from jax import lax
 from jax.sharding import PartitionSpec as P
+
+
+def turned_line(block, axis, dim):
+    size = lax.axis_size(axis)
+    forward = [(i, (i + 1) % size) for i in range(size)]
+    parts = [block]
+    for stride in range(1, size):
+        parts = [lax.ppermute(parts[0], axis, forward), *parts]
+    whole = jnp.concatenate(parts, axis=dim)
+    shift = (lax.axis_index(axis) + 1) * parts[-1].shape[dim]
+    return jnp.roll(whole, shift, axis=dim)
 
 
 def padded_2(cells, sides, width):
@@ -92,7 +103,7 @@
     count, top_depth, top_rows, top_cols = top_in.shape
     along_x = lax.all_gather(top_in, "gx", axis=3, tiled=True)
     along_y = lax.all_gather(along_x, "gy", axis=2, tiled=True)
-    along_z = lax.all_gather(along_y, "gz", axis=1, tiled=True)
+    along_z = turned_line(along_y, "gz", 1)
     whole_top = along_z.reshape(count, -1)
     kernel_rows = top_kernel.reshape(-1, top_kernel.shape[3])
     top_part = lax.dot_general(

time: 187 us -> 181 us (0.968)
  blocking collectives: 25.3 us -> 13.2 us
  starting transfers between devices: 31.9 us -> 34.8 us
    all_gather x1 -> x0, blocking collectives: 13.6 us -> none  [shards(): along_z = lax.all_gather(along_y, 'gz', axis=1, tiled=True)]
    ppermute x0 -> x3, starting transfers between devices: none -> 4.87 us  [turned_line(): parts = [lax.ppermute(parts[0], axis, forward), *parts]]
    ppermute x6, starting transfers between devices: 24 us -> 22 us  [padded_2(): lax.ppermute(tail, axis, [(i, (i + 1) % count) for i in range(ends)])]
    slice x6, local copies, waits for them, and re-layouts: 3.37 us -> 5.26 us  [padded_2(): lax.slice_in_dim(cells, cells.shape[dim] - width, cells.shape[dim], axis=...]
    unnamed x14 -> x29, local copies, waits for them, and re-layouts: 5.63 us -> 5.62 us
  transfers between devices with their start and end apart: 12 -> 15, of which waited for: 0 -> 1; matrix products, arithmetic and copies ran while one was open for 49% -> 53% of each run, Pallas kernels for 0% -> 0%
where the time goes in v1:
time: 181 us; the launch traced here: 178 us
  local copies, waits for them, and re-layouts  66.3 us (37%)
  other arithmetic  46.2 us (26%)
  starting transfers between devices  34.8 us (19%)
  matrix products  16.7 us (9%)
  blocking collectives  13.2 us (7%)
    ppermute x6, starting transfers between devices, padded_2(): lax.ppermute(tail, axis, [(i, (i + 1) % count) for i in range(ends)])  22 us
    dot_general x2, matrix products, conv_padded(): lax.dot_general(padded, band, (((along,), (0,)), ((), ())), precision=lax...  16.3 us
    reshape x2, local copies, waits for them, and re-layouts, prolong(): return jnp.repeat(values, factor, axis=3)  13.6 us
    reduce_sum x2, other arithmetic, restrict(): return shaped.mean(axis=(2, 4, 6))  12.3 us
    broadcast_in_dim x2, local copies, waits for them, and re-layouts, prolong(): return jnp.repeat(values, factor, axis=3)  12.2 us
    all_gather x1, blocking collectives, shards(): along_x = lax.all_gather(top_in, 'gx', axis=3, tiled=True)  11.4 us
    add x1, other arithmetic, conv_padded(): total + kernel_row[offset] * lax.slice_in_dim(padded, offset, offset + le...  10.5 us
    convert_element_type x1, other arithmetic, shards(): return (fine_part + prolong(coarse_total, 2)).astype(jnp.bfloat16)  10.3 us
  transfers between devices with their start and end apart: 15, of which 1 were waited for; matrix products, arithmetic and copies ran while one was open for 53% of the time, Pallas kernels for 0%

profile of v1, /device:TPU:0, one launch (start us, length us, event | category | flops | bytes accessed | tf_op | source)
XLA Modules:
  0.0 177.9 jit_solution(6073491595189725051)
XLA Ops:
  0.0 9.9 %copy.23 = f32[16,16,16,128]{0,3,2,1:T(8,128)} copy(bf16[16,16,16,128]{3,2,1,0:T(8,128)(2,1)} %param.4) | data formatting | bytes 3145728 | tf_op jit(solution)/shard_map/reshape | solution.py:73
  9.9 11.7 %reduce_sum.18 = f32[16,8,8,64]{0,3,2,1:T(8,128)S(1)} reduce(f32[16,8,2,8,2,64,2]{0,6,5,4,3,2,1:T(2,128)} %bitcast.77, f32[]{:T(128)} %constant.17.clone.1), dimensions={2,4,6}, to_apply=%region_0.0 | reduce | flops 458752 | bytes 2359300 | tf_op jit(solution)/shard_map/reduce_sum | solution.py:76
  21.7 0.6 copy.24
  22.3 0.9 fusion.209
  23.2 0.9 fusion.215
  24.1 5.6 %collective-permute-start.6 = (bf16[16,8,8,4]{3,0,2,1:T(8,128)(2,1)}, bf16[16,8,8,4]{3,0,2,1:T(8,128)(2,1)}, u32[]{:S(2)}, u32[]{:S(2)}) collective-permute-start(bf16[16,8,8,4]{3,0,2,1:T(8,128)(2,1)} %get-tuple-element.17), channel_id=1, source_target_pairs={{0,8},{8,16},{16,24},{1,9},{9,17},{17,25},{2,10},{10,18},{18,26},{... | collective-permute-start | bytes 24584 | tf_op jit(solution)/shard_map/ppermute | solution.py:26
  29.7 1.3 collective-permute-start.7
  31.0 1.7 copy.25
  32.7 0.5 reduce_sum.19
  33.3 11.4 %all_gather.6 = bf16[16,2,2,64]{0,2,1,3:T(2,128)(2,1)S(1)} all-gather(bf16[16,2,2,16]{0,2,1,3:T(2,128)(2,1)S(1)} %copy.26), channel_id=1, replica_groups=mesh['gx'=4,'gy'=2,'gz'=4] {'gx'}, dimensions={3}, use_global_device_ids=true | all-gather | bytes 10240 | tf_op jit(solution)/shard_map/all_gather | solution.py:104
  44.7 0.1 copy.27
  44.8 1.8 %all_gather.7 = bf16[16,2,4,64]{3,0,1,2:T(8,128)(2,1)S(1)} all-gather(bf16[16,2,2,64]{3,0,1,2:T(8,128)(2,1)S(1)} %copy.27), channel_id=1, replica_groups=mesh['gx'=4,'gy'=2,'gz'=4] {'gy'}, dimensions={2}, use_global_device_ids=true | all-gather | bytes 24576 | tf_op jit(solution)/shard_map/all_gather | solution.py:105
  46.6 1.6 collective-permute-start.12
  48.2 1.6 fusion.212
  49.8 3.0 %copy.37 = bf16[16,16,16,4]{2,1,3,0:T(8,128)(2,1)S(1)} copy(bf16[16,16,16,4]{3,2,1,0:T(8,128)(2,1)} %get-tuple-element.9) | data formatting | bytes 65536
  52.8 3.7 %collective-permute-start = (bf16[16,16,16,4]{2,1,3,0:T(8,128)(2,1)S(1)}, bf16[16,16,16,4]{2,1,3,0:T(8,128)(2,1)S(1)}, u32[]{:S(2)}, u32[]{:S(2)}) collective-permute-start(bf16[16,16,16,4]{2,1,3,0:T(8,128)(2,1)S(1)} %copy.37), channel_id=1, source_target_pairs={{0,8},{8,16},{16,24},{1,9},{9,17},{17,25},{2,10},{10,18},{18,26},{... | collective-permute-start | bytes 98312 | tf_op jit(solution)/shard_map/ppermute | solution.py:26
  56.5 1.7 copy.38
  58.2 1.3 collective-permute-start.1
  59.6 0.7 fusion.218
  60.3 0.7 fusion.219
  61.0 0.7 fusion.216
  61.7 0.7 fusion.217
  62.4 7.0 %convolution_convert_fusion = bf16[16,8,8,64]{3,0,2,1:T(8,128)(2,1)S(1)} fusion(bf16[16,8,8,4]{3,0,2,1:T(8,128)(2,1)} %collective-permute-done.7, bf16[16,8,8,64]{3,0,2,1:T(8,128)(2,1)S(1)} %copy-done.6, bf16[16,8,8,4]{3,0,2,1:T(8,128)(2,1)} %collective-permute-done.6, f32[]{:T(128)} %bitcast.40, f32[]{:T(128)} %bitcast.39, f32[]{:T(128)} %bitcast.38, ...), kind=kOutput, calls=%fused_computation.80 | convolution fusion | flops 57255424 | bytes 278564 | tf_op jit(solution)/shard_map/dot_general | solution.py:50
  69.3 0.7 fusion.214
  70.1 1.5 collective-permute-start.8
  71.5 1.3 collective-permute-start.9
  72.8 1.6 collective-permute-start.13
  74.5 1.6 copy.21
  76.1 3.5 %copy.22 = bf16[16,16,16,4]{3,2,1,0:T(8,128)(2,1)} copy(bf16[16,16,16,4]{2,1,3,0:T(8,128)(2,1)} %collective-permute-done.1) | data formatting | bytes 65536 | tf_op jit(solution)/shard_map/ppermute | solution.py:28
  79.6 9.3 %fusion.46 = f32[16,16,16,128]{3,2,1,0:T(8,128)S(1)} fusion(bf16[16,16,16,4]{3,2,1,0:T(8,128)(2,1)} %copy.22, bf16[16,16,16,128]{3,2,1,0:T(8,128)(2,1)S(1)} %copy-done.2, bf16[16,16,16,4]{3,2,1,0:T(8,128)(2,1)S(1)} %copy.21, f32[]{:T(128)} %bitcast.10, f32[]{:T(128)} %bitcast.9, f32[]{:T(128)} %bitcast.8, f32[]{:T(128)} %bitcast.7, f32[]{:T(128)} %bitcast.6, ...), kind=kOutput, calls=%fused_computation.74 | convolution fusion | flops 859450368 | bytes 3211300 | tf_op jit(solution)/shard_map/dot_general | solution.py:50
  88.9 1.6 collective-permute-start.14
  90.5 0.3 fusion.211
  90.8 2.5 %collective-permute-start.2 = (f32[16,16,4,128]{3,2,1,0:T(4,128)S(1)}, f32[16,16,4,128]{3,2,1,0:T(4,128)S(1)}, u32[]{:S(2)}, u32[]{:S(2)}) collective-permute-start(f32[16,16,4,128]{3,2,1,0:T(4,128)S(1)} %get-tuple-element.7), channel_id=1, source_target_pairs={{0,4},{1,5},{2,6},{3,7},{8,12},{9,13},{10,14},{11,15},{16,20},{17,... | collective-permute-start | bytes 1572872 | tf_op jit(solution)/shard_map/ppermute | solution.py:26
  93.3 1.5 collective-permute-start.3
  94.8 0.1 collective-permute-done.14
  95.0 0.1 copy.28
  95.1 0.2 reshape.156
  95.3 0.2 maximum_convert_fusion
  95.5 6.1 %fusion.62 = bf16[16,8,8,64]{3,0,2,1:T(8,128)(2,1)S(1)} fusion(f32[16,8,16,64]{3,0,2,1:T(8,128)S(1)} %maximum_convert_fusion, f32[]{:T(128)} %bitcast.50, f32[]{:T(128)} %bitcast.49, f32[]{:T(128)} %bitcast.48, f32[]{:T(128)} %bitcast.47, f32[]{:T(128)} %bitcast.46, f32[]{:T(128)} %bitcast.45, f32[]{:T(128)} %bitcast.44, f32[]{:T(128)} %bitcast.43, f32[]{:T(128)} %bitcast.30), kind=kLoop, calls=%fused_computation.101 | loop fusion | flops 1179648 | bytes 2490404 | tf_op jit(solution)/shard_map/convert_element_type | solution.py:100
  101.6 0.7 fusion.213
  102.3 3.4 %collective-permute-start.10 = (bf16[16,4,8,64]{3,0,2,1:T(8,128)(2,1)}, bf16[16,4,8,64]{3,0,2,1:T(8,128)(2,1)S(1)}, u32[]{:S(2)}, u32[]{:S(2)}) collective-permute-start(bf16[16,4,8,64]{3,0,2,1:T(8,128)(2,1)} %get-tuple-element.13), channel_id=1, source_target_pairs={{0,1},{1,2},{2,3},{4,5},{5,6},{6,7},{8,9},{9,10},{10,11},{12,13},{... | collective-permute-start | bytes 196616 | tf_op jit(solution)/shard_map/ppermute | solution.py:26
  105.7 1.3 collective-permute-start.11
  107.1 0.0 copy-start.7
  107.1 0.8 copy-done.7
  107.9 10.5 %fusion.25 = f32[16,16,16,128]{3,2,1,0:T(8,128)S(1)} fusion(f32[16,16,16,128]{3,2,1,0:T(8,128)S(1)} %copy-done.4, f32[16,16,4,128]{3,2,1,0:T(4,128)} %copy-done.7, f32[16,16,4,128]{3,2,1,0:T(4,128)S(1)} %collective-permute-done.2, f32[]{:T(128)} %bitcast.20, f32[]{:T(128)} %bitcast.19, f32[]{:T(128)} %bitcast.18, f32[]{:T(128)} %bitcast.17, f32[]{:T(128)} %bitcast.16, ...), kind=kLoop, calls=%fused_computation.49 | loop fusion | flops 13107200 | bytes 5242916 | tf_op jit(solution)/shard_map/add | solution.py:59
  118.4 1.0 fusion.210
  119.5 5.3 %collective-permute-start.4 = (f32[16,4,16,128]{3,2,1,0:T(8,128)}, f32[16,4,16,128]{3,2,1,0:T(8,128)}, u32[]{:S(2)}, u32[]{:S(2)}) collective-permute-start(f32[16,4,16,128]{3,2,1,0:T(8,128)} %get-tuple-element.5), channel_id=1, source_target_pairs={{0,1},{1,2},{2,3},{4,5},{5,6},{6,7},{8,9},{9,10},{10,11},{12,13},{... | collective-permute-start | bytes 1572872 | tf_op jit(solution)/shard_map/ppermute | solution.py:26
  124.8 1.3 collective-permute-start.5
  126.1 0.4 fusion.111
  126.5 0.1 copy.29
  126.6 0.1 broadcast_in_dim.118
  126.6 0.1 broadcast_in_dim.119
  126.7 1.5 broadcast_in_dim.120
  128.2 2.2 %copy.30 = f32[16,8,8,64]{3,0,2,1:T(8,128)S(1)} copy(f32[16,8,8,64]{0,2,3,1:T(8,128)} %bitcast.79) | data formatting | bytes 524288 | tf_op jit(solution)/shard_map/reshape | solution.py:82
  130.4 0.0 collective-permute-done.11
  130.4 0.2 maximum_convert_fusion.1
  130.6 5.8 %fusion.53 = f32[16,8,8,64]{3,0,2,1:T(8,128)S(1)} fusion(f32[16,8,8,64]{3,0,2,1:T(8,128)S(1)} %copy.30, f32[16,16,8,64]{3,0,2,1:T(8,128)S(1)} %maximum_convert_fusion.1, f32[]{:T(128)} %bitcast.58, f32[]{:T(128)} %bitcast.57, f32[]{:T(128)} %bitcast.56, f32[]{:T(128)} %bitcast.55, f32[]{:T(128)} %bitcast.54, f32[]{:T(128)} %bitcast.53, f32[]{:T(128)} %bitcast.52, ...), kind=kLoop, calls=%fused_computation.83 | loop fusion | flops 1179648 | bytes 2883620 | tf_op jit(solution)/shard_map/add | solution.py:113
  136.4 0.3 copy.31
  136.7 0.4 broadcast_in_dim.121
  137.1 1.5 broadcast_in_dim.122
  138.6 6.7 %copy.32 = f32[16,16,16,64]{2,1,3,0:T(8,128)} copy(f32[16,16,16,64]{3,1,2,0:T(8,128)} %bitcast.80) | data formatting | bytes 2097152 | tf_op jit(solution)/shard_map/reshape | solution.py:81
  145.3 10.7 %broadcast_in_dim.123 = f32[16,16,16,64,2]{2,1,4,3,0:T(8,128)} broadcast(f32[16,16,16,64]{2,1,3,0:T(8,128)} %copy.32), dimensions={0,1,2,3} | broadcast | bytes 3145728 | tf_op jit(solution)/shard_map/broadcast_in_dim | solution.py:82
  156.0 11.4 %copy.33 = f32[16,16,16,128]{3,2,1,0:T(8,128)} copy(f32[16,16,16,128]{2,1,3,0:T(8,128)} %bitcast.76) | data formatting | bytes 4194304 | tf_op jit(solution)/shard_map/reshape | solution.py:82
  167.4 10.3 %fusion.5 = bf16[16,16,16,128]{3,2,1,0:T(8,128)(2,1)} fusion(f32[16,16,16,128]{3,2,1,0:T(8,128)} %copy.33, f32[16,16,16,128]{3,2,1,0:T(8,128)S(1)} %fusion.25, f32[16,4,16,128]{3,2,1,0:T(8,128)} %collective-permute-done.5, f32[16,4,16,128]{3,2,1,0:T(8,128)} %collective-permute-done.4, f32[]{:T(128)} %bitcast.28, f32[]{:T(128)} %bitcast.27, f32[]{:T(128)} %bitcast.26, ...), kind=kLoop, calls=%fused_computation.29 | loop fusion | flops 14155776 | bytes 6291492 | tf_op jit(solution)/shard_map/convert_element_type | solution.py:114
  (42 shorter events, 0.2 us)
Async XLA Ops:
  0.0 126.1 %copy-start = (bf16[2,2,16,2048]{3,2,1,0:T(8,128)(2,1)S(1)}, bf16[2,2,16,2048]{3,2,1,0:T(8,128)(2,1)}, u32[]{:S(2)}) copy-start(bf16[2,2,16,2048]{3,2,1,0:T(8,128)(2,1)} %param.7) | copy-start | bytes 786436
  23.2 7.8 %copy-start.5 = (bf16[16,8,8,64]{3,0,2,1:T(8,128)(2,1)}, bf16[16,8,8,64]{3,0,2,1:T(8,128)(2,1)S(1)}, u32[]{:S(2)}) copy-start(bf16[16,8,8,64]{3,0,2,1:T(8,128)(2,1)S(1)} %get-tuple-element.11) | copy-start | bytes 393220
  24.1 38.3 %collective-permute-start.6 = (bf16[16,8,8,4]{3,0,2,1:T(8,128)(2,1)}, bf16[16,8,8,4]{3,0,2,1:T(8,128)(2,1)}, u32[]{:S(2)}, u32[]{:S(2)}) collective-permute-start(bf16[16,8,8,4]{3,0,2,1:T(8,128)(2,1)} %get-tuple-element.17), channel_id=1, source_target_pairs={{0,8},{8,16},{16,24},{1,9},{9,17},{17,25},{2,10},{10,18},{18,26},{... | collective-permute-start | bytes 24584 | tf_op jit(solution)/shard_map/ppermute | solution.py:26
  29.7 32.7 %collective-permute-start.7 = (bf16[16,8,8,4]{3,0,2,1:T(8,128)(2,1)}, bf16[16,8,8,4]{3,0,2,1:T(8,128)(2,1)}, u32[]{:S(2)}, u32[]{:S(2)}) collective-permute-start(bf16[16,8,8,4]{3,0,2,1:T(8,128)(2,1)} %get-tuple-element.18), channel_id=1, source_target_pairs={{8,0},{16,8},{24,16},{9,1},{17,9},{25,17},{10,2},{18,10},{26,18},{... | collective-permute-start | bytes 24584 | tf_op jit(solution)/shard_map/ppermute | solution.py:28
  31.0 17.2 %copy-start.2 = (bf16[16,16,16,128]{3,2,1,0:T(8,128)(2,1)S(1)}, bf16[16,16,16,128]{3,2,1,0:T(8,128)(2,1)}, u32[]{:S(2)}) copy-start(bf16[16,16,16,128]{3,2,1,0:T(8,128)(2,1)} %param.4) | copy-start | bytes 3145732
  46.6 26.2 %collective-permute-start.12 = (bf16[16,2,4,64]{3,0,1,2:T(8,128)(2,1)S(1)}, bf16[16,2,4,64]{3,0,1,2:T(8,128)(2,1)S(1)}, u32[]{:S(2)}, u32[]{:S(2)}) collective-permute-start(bf16[16,2,4,64]{3,0,1,2:T(8,128)(2,1)S(1)} %all_gather.7), channel_id=1, source_target_pairs={{0,1},{1,2},{2,3},{3,0},{4,5},{5,6},{6,7},{7,4},{8,9},{9,10},{10,1... | collective-permute-start | bytes 49160 | tf_op jit(solution)/shard_map/ppermute | solution.py:12
  49.8 9.8 %copy-start.8 = (f32[3,9]{1,0:T(4,128)S(1)}, f32[3,9]{1,0:T(4,128)}, u32[]{:S(2)}) copy-start(f32[3,9]{1,0:T(4,128)} %param.6) | copy-start | bytes 328
  49.8 11.2 %copy-start.9 = (f32[3,9]{1,0:T(4,128)S(1)}, f32[3,9]{1,0:T(4,128)}, u32[]{:S(2)}) copy-start(f32[3,9]{1,0:T(4,128)} %param.5) | copy-start | bytes 328
  49.8 12.6 %copy-start.6 = (bf16[16,8,8,64]{3,0,2,1:T(8,128)(2,1)S(1)}, bf16[16,8,8,64]{3,0,2,1:T(8,128)(2,1)}, u32[]{:S(2)}) copy-start(bf16[16,8,8,64]{3,0,2,1:T(8,128)(2,1)} %copy-done.5) | copy-start | bytes 393220
  52.8 21.7 %collective-permute-start = (bf16[16,16,16,4]{2,1,3,0:T(8,128)(2,1)S(1)}, bf16[16,16,16,4]{2,1,3,0:T(8,128)(2,1)S(1)}, u32[]{:S(2)}, u32[]{:S(2)}) collective-permute-start(bf16[16,16,16,4]{2,1,3,0:T(8,128)(2,1)S(1)} %copy.37), channel_id=1, source_target_pairs={{0,8},{8,16},{16,24},{1,9},{9,17},{17,25},{2,10},{10,18},{18,26},{... | collective-permute-start | bytes 98312 | tf_op jit(solution)/shard_map/ppermute | solution.py:26
  58.2 17.8 %collective-permute-start.1 = (bf16[16,16,16,4]{2,1,3,0:T(8,128)(2,1)S(1)}, bf16[16,16,16,4]{2,1,3,0:T(8,128)(2,1)}, u32[]{:S(2)}, u32[]{:S(2)}) collective-permute-start(bf16[16,16,16,4]{2,1,3,0:T(8,128)(2,1)S(1)} %copy.38), channel_id=1, source_target_pairs={{8,0},{16,8},{24,16},{9,1},{17,9},{25,17},{10,2},{18,10},{26,18},{... | collective-permute-start | bytes 98312 | tf_op jit(solution)/shard_map/ppermute | solution.py:28
  70.1 25.2 %collective-permute-start.8 = (bf16[16,8,4,64]{3,0,2,1:T(8,128)(2,1)}, bf16[16,8,4,64]{3,0,2,1:T(8,128)(2,1)S(1)}, u32[]{:S(2)}, u32[]{:S(2)}) collective-permute-start(bf16[16,8,4,64]{3,0,2,1:T(8,128)(2,1)} %get-tuple-element.15), channel_id=1, source_target_pairs={{0,4},{1,5},{2,6},{3,7},{8,12},{9,13},{10,14},{11,15},{16,20},{17,... | collective-permute-start | bytes 196616 | tf_op jit(solution)/shard_map/ppermute | solution.py:26
  71.5 23.8 %collective-permute-start.9 = (bf16[16,8,4,64]{3,0,2,1:T(8,128)(2,1)}, bf16[16,8,4,64]{3,0,2,1:T(8,128)(2,1)S(1)}, u32[]{:S(2)}, u32[]{:S(2)}) collective-permute-start(bf16[16,8,4,64]{3,0,2,1:T(8,128)(2,1)} %get-tuple-element.16), channel_id=1, source_target_pairs={{4,0},{5,1},{6,2},{7,3},{12,8},{13,9},{14,10},{15,11},{20,16},{21,... | collective-permute-start | bytes 196616 | tf_op jit(solution)/shard_map/ppermute | solution.py:28
  72.8 16.0 %collective-permute-start.13 = (bf16[16,2,4,64]{3,0,1,2:T(8,128)(2,1)S(1)}, bf16[16,2,4,64]{3,0,1,2:T(8,128)(2,1)S(1)}, u32[]{:S(2)}, u32[]{:S(2)}) collective-permute-start(bf16[16,2,4,64]{3,0,1,2:T(8,128)(2,1)S(1)} %collective-permute-done.12), channel_id=1, source_target_pairs={{0,1},{1,2},{2,3},{3,0},{4,5},{5,6},{6,7},{7,4},{8,9},{9,10},{10,1... | collective-permute-start | bytes 49160 | tf_op jit(solution)/shard_map/ppermute | solution.py:12
  88.9 1.6 copy-start.3
  88.9 6.0 %collective-permute-start.14 = (bf16[16,2,4,64]{3,0,1,2:T(8,128)(2,1)S(1)}, bf16[16,2,4,64]{3,0,1,2:T(8,128)(2,1)S(1)}, u32[]{:S(2)}, u32[]{:S(2)}) collective-permute-start(bf16[16,2,4,64]{3,0,1,2:T(8,128)(2,1)S(1)} %collective-permute-done.13), channel_id=1, source_target_pairs={{0,1},{1,2},{2,3},{3,0},{4,5},{5,6},{6,7},{7,4},{8,9},{9,10},{10,1... | collective-permute-start | bytes 49160 | tf_op jit(solution)/shard_map/ppermute | solution.py:12
  90.8 16.3 %collective-permute-start.2 = (f32[16,16,4,128]{3,2,1,0:T(4,128)S(1)}, f32[16,16,4,128]{3,2,1,0:T(4,128)S(1)}, u32[]{:S(2)}, u32[]{:S(2)}) collective-permute-start(f32[16,16,4,128]{3,2,1,0:T(4,128)S(1)} %get-tuple-element.7), channel_id=1, source_target_pairs={{0,4},{1,5},{2,6},{3,7},{8,12},{9,13},{10,14},{11,15},{16,20},{17,... | collective-permute-start | bytes 1572872 | tf_op jit(solution)/shard_map/ppermute | solution.py:26
  93.3 13.7 %collective-permute-start.3 = (f32[16,16,4,128]{3,2,1,0:T(4,128)S(1)}, f32[16,16,4,128]{3,2,1,0:T(4,128)S(1)}, u32[]{:S(2)}, u32[]{:S(2)}) collective-permute-start(f32[16,16,4,128]{3,2,1,0:T(4,128)S(1)} %get-tuple-element.8), channel_id=1, source_target_pairs={{4,0},{5,1},{6,2},{7,3},{12,8},{13,9},{14,10},{15,11},{20,16},{21,... | collective-permute-start | bytes 1572872 | tf_op jit(solution)/shard_map/ppermute | solution.py:28
  95.5 12.4 %copy-start.4 = (f32[16,16,16,128]{3,2,1,0:T(8,128)S(1)}, f32[16,16,16,128]{3,2,1,0:T(8,128)}, u32[]{:S(2)}) copy-start(f32[16,16,16,128]{3,2,1,0:T(8,128)} %copy-done.3) | copy-start | bytes 6291460
  102.3 28.1 %collective-permute-start.10 = (bf16[16,4,8,64]{3,0,2,1:T(8,128)(2,1)}, bf16[16,4,8,64]{3,0,2,1:T(8,128)(2,1)S(1)}, u32[]{:S(2)}, u32[]{:S(2)}) collective-permute-start(bf16[16,4,8,64]{3,0,2,1:T(8,128)(2,1)} %get-tuple-element.13), channel_id=1, source_target_pairs={{0,1},{1,2},{2,3},{4,5},{5,6},{6,7},{8,9},{9,10},{10,11},{12,13},{... | collective-permute-start | bytes 196616 | tf_op jit(solution)/shard_map/ppermute | solution.py:26
  105.7 24.7 %collective-permute-start.11 = (bf16[16,4,8,64]{3,0,2,1:T(8,128)(2,1)}, bf16[16,4,8,64]{3,0,2,1:T(8,128)(2,1)S(1)}, u32[]{:S(2)}, u32[]{:S(2)}) collective-permute-start(bf16[16,4,8,64]{3,0,2,1:T(8,128)(2,1)} %get-tuple-element.14), channel_id=1, source_target_pairs={{1,0},{2,1},{3,2},{5,4},{6,5},{7,6},{9,8},{10,9},{11,10},{13,12},{... | collective-permute-start | bytes 196616 | tf_op jit(solution)/shard_map/ppermute | solution.py:28
  107.1 0.8 copy-start.7
  119.5 47.9 %collective-permute-start.4 = (f32[16,4,16,128]{3,2,1,0:T(8,128)}, f32[16,4,16,128]{3,2,1,0:T(8,128)}, u32[]{:S(2)}, u32[]{:S(2)}) collective-permute-start(f32[16,4,16,128]{3,2,1,0:T(8,128)} %get-tuple-element.5), channel_id=1, source_target_pairs={{0,1},{1,2},{2,3},{4,5},{5,6},{6,7},{8,9},{9,10},{10,11},{12,13},{... | collective-permute-start | bytes 1572872 | tf_op jit(solution)/shard_map/ppermute | solution.py:26
  124.8 42.6 %collective-permute-start.5 = (f32[16,4,16,128]{3,2,1,0:T(8,128)}, f32[16,4,16,128]{3,2,1,0:T(8,128)}, u32[]{:S(2)}, u32[]{:S(2)}) collective-permute-start(f32[16,4,16,128]{3,2,1,0:T(8,128)} %get-tuple-element.6), channel_id=1, source_target_pairs={{1,0},{2,1},{3,2},{5,4},{6,5},{7,6},{9,8},{10,9},{11,10},{13,12},{... | collective-permute-start | bytes 1572872 | tf_op jit(solution)/shard_map/ppermute | solution.py:28
  167.4 10.3 %copy-start.1 = (bf16[2,2,16,2048]{3,2,1,0:T(8,128)(2,1)S(1)}, bf16[2,2,16,2048]{3,2,1,0:T(8,128)(2,1)}, u32[]{:S(2)}) copy-start(bf16[2,2,16,2048]{3,2,1,0:T(8,128)(2,1)} %param.7) | copy-start | bytes 786436
